TPU v7x, 512 devices: a whole 4x4x16 slice. The times are simulated.
512 devices in a mesh: walk: 8 (over x, core), chol: 64 (over z, y).
Axes of the slice: x: 4, y: 4, z: 16, core: 2. Of those that a mesh axis runs over, the one named last changes fastest.
Arguments:
- walkers: bfloat16 [64, 2048, 256], P('walk', 'chol'), may hold values from -2.5 to 2.5
- trial: bfloat16 [2048, 256], P('chol'), may hold values from -1.05 to 1.05
- cholesky: bfloat16 [32, 2048, 2048], P(None, 'chol'), may hold values from -0.125 to 0.125
- rotated: bfloat16 [32, 2048, 256], P(None, 'chol'), may hold values from -0.09375 to 0.09375
- fields: float32 [64, 32], P('walk'), may hold values from -4 to 4
- source: int32 [64], replicated, may hold values from 0 to 63, as said below
Outputs:
- propagated: bfloat16 [64, 2048, 256], P('walk', 'chol')
- force_bias: float32 [64, 32], P('walk')
Inputs may be any that keep to these rules, and one draw needn't show every extreme that they name: source is a permutation of the walkers. New slots g * 8 to (g + 1) * 8 - 1 form group g, as do the old walkers. Of the old walkers of one group at most 4 fill slots of any one new group, and in every draw some group sends exactly 4 to some group.
All inputs are finite; a program needn't handle non-finite values.
Results may differ from a plain program's by a relative error of at most 0.0051.
Values may be sent and summed in bfloat16 or wider, within the bound.
A program may use at most 128 MiB of HBM per device.

v0:
```python
import jax
import jax.numpy as jnp
from jax import lax
from jax.sharding import Mesh
from jax.sharding import PartitionSpec as P

ITERS = 3
CHOL = ("chol_0", "chol_1")


TAU_ROOT = 0.1


def rows_first(arrays, axis, dims):
    turned = [jnp.moveaxis(a, dim, 0) for a, dim in zip(arrays, dims)]
    widths = [t[0].size for t in turned]
    both = jnp.concatenate([t.reshape(-1, w) for t, w in zip(turned, widths)], axis=1)
    out = lax.all_gather(both, axis, axis=0, tiled=True)
    pieces = jnp.split(out, [sum(widths[:k]) for k in range(1, len(widths))], axis=1)
    return tuple(
        (
            jnp.moveaxis(b.reshape(-1, *t.shape[1:]), 0, dim)
            for b, t, dim in zip(pieces, turned, dims)
        )
    )


def copy_for_each(array, axis):
    copies = jnp.broadcast_to(array, (lax.axis_size(axis), *array.shape))
    return lax.all_to_all(copies, axis, split_axis=0, concat_axis=0, tiled=True)


def taken_together(array, axis):
    return copy_for_each(array, axis).sum(axis=0)


def gather_axes(array, axes, dim):
    out = array
    for number in range(len(axes) - 1, -1, -1):
        out = lax.all_gather(out, axes[number], axis=dim, tiled=True)
    return out


def newton_inverse(intersections):
    identity = jnp.eye(intersections.shape[-1], dtype=jnp.float32)
    estimate = jnp.broadcast_to(identity, intersections.shape)
    for sweep_index in range(ITERS):
        product = jnp.einsum(
            "wij,wjk->wik", intersections, estimate, precision=lax.Precision.HIGHEST
        )
        estimate = jnp.einsum(
            "wij,wjk->wik", estimate, 2.0 * identity - product, precision=lax.Precision.HIGHEST
        )
    return estimate


def column_fold(potential, shard_piece):
    return jnp.einsum("wpq,wqi->wpi", potential, shard_piece, preferred_element_type=jnp.float32)


def shards(walkers, trial, cholesky, rotated, fields, source):
    per_group = walkers.shape[0]
    row_count = walkers.shape[1]
    electrons = walkers.shape[2]
    group_index = lax.axis_index("walk")
    group_count = lax.axis_size("walk")
    capacity = per_group // 2
    anchor = (source // per_group).reshape(group_count, per_group)
    local_slot = (source % per_group).reshape(group_count, per_group)
    from_here = (anchor == group_index).astype(jnp.int32)
    before = jnp.cumsum(from_here, axis=1) - from_here
    slot_match = (from_here[:, None, :] == 1) & (
        before[:, None, :] == jnp.arange(capacity)[None, :, None]
    )
    picked = jnp.sum(jnp.where(slot_match, local_slot[:, None, :], 0), axis=2)
    filled = jnp.any(slot_match, axis=2)
    outgoing = jnp.take(walkers, picked.reshape(-1), axis=0).reshape(
        group_count, capacity, row_count, electrons
    )
    outgoing = jnp.where(filled[:, :, None, None], outgoing, jnp.zeros_like(outgoing))
    arrived = lax.all_to_all(outgoing, "walk", split_axis=0, concat_axis=0, tiled=True)
    arrived = arrived.reshape(group_count * capacity, row_count, electrons)
    incoming_groups = (
        lax.dynamic_slice_in_dim(source, group_index * per_group, per_group) // per_group
    )
    positions = jnp.arange(per_group)
    same_anchor = (incoming_groups[:, None] == incoming_groups[None, :]) & (
        positions[None, :] < positions[:, None]
    )
    order_rank = jnp.sum(same_anchor.astype(jnp.int32), axis=1)
    migrated = jnp.take(arrived, incoming_groups * capacity + order_rank, axis=0)
    gathered, gathered_trial = rows_first((migrated, trial), CHOL, (1, 0))
    intersections = jnp.einsum(
        "pi,wpj->wij", gathered_trial, gathered, preferred_element_type=jnp.float32
    )
    inverse = newton_inverse(intersections).astype(jnp.bfloat16)
    greens = jnp.einsum(
        "wpj,wji->wpi", migrated, inverse, preferred_element_type=jnp.float32
    ).astype(jnp.bfloat16)
    vectors = rotated.shape[0]
    partial_bias = lax.dot_general(
        greens.reshape(per_group, -1),
        rotated.reshape(vectors, -1),
        (((1,), (1,)), ((), ())),
        preferred_element_type=jnp.float32,
    )
    force_bias = TAU_ROOT * taken_together(partial_bias, CHOL)
    shifted = (fields - force_bias).astype(jnp.bfloat16)
    potential = (
        TAU_ROOT
        * jnp.dot(shifted, cholesky.reshape(vectors, -1), preferred_element_type=jnp.float32)
    ).astype(jnp.bfloat16)
    potential = potential.reshape(per_group, row_count, -1)
    first_term = jnp.einsum("wpq,wqi->wpi", potential, gathered, preferred_element_type=jnp.float32)
    second_term = column_fold(potential, gather_axes(first_term.astype(jnp.bfloat16), CHOL, 1))
    propagated = (migrated.astype(jnp.float32) + first_term + 0.5 * second_term).astype(
        jnp.bfloat16
    )
    return (propagated, force_bias)


def solution(mesh):
    split = Mesh(mesh.devices.reshape(mesh.shape["walk"], 16, 4), ("walk", "chol_0", "chol_1"))
    placed = (
        P("walk", CHOL, None),
        P(CHOL, None),
        P(None, CHOL, None),
        P(None, CHOL, None),
        P("walk", None),
        P(),
    )
    return jax.shard_map(
        shards,
        mesh=split,
        in_specs=placed,
        out_specs=(P("walk", CHOL, None), P("walk", None)),
        check_vma=False,
    )
```

profile of v0, /device:TPU:6, one launch (start us, length us, event | category | flops | bytes accessed | tf_op | source)
XLA Modules:
  0.0 389.2 jit_solution(3932483497098475337)
XLA Ops:
  7.2 0.0 copy-start
  7.2 0.0 copy-start.4
  7.2 0.0 copy-start.2
  7.2 0.7 and_select_fusion
  7.9 0.7 compare_convert_fusion
  8.6 0.1 reshape.112
  8.7 0.2 reduce_window_sum.11
  8.8 0.1 broadcast_in_dim.68
  8.9 0.2 select_reduce_fusion
  9.1 0.1 copy.35
  9.2 0.2 fusion.27
  9.3 0.1 reshape.106
  9.4 0.1 copy.34
  9.5 0.1 copy.33
  9.6 1.5 gather_fusion
  11.1 0.9 select_select_fusion
  12.0 9.3 %all-to-all-start = ((bf16[8,4,32,256]{3,2,1,0:T(8,128)(2,1)}), bf16[8,4,32,256]{3,2,1,0:T(8,128)(2,1)S(1)}, u32[]{:S(2)}, u32[]{:S(2)}) async-start(bf16[8,4,32,256]{3,2,1,0:T(8,128)(2,1)} %select_select_fusion), calls=%async_computation | async-start | bytes 1048576 | tf_op jit(solution)/shard_map/all_to_all | solution.py:81
  21.3 0.0 all-gather.3.cloned.1.call-start
  21.3 0.0 copy-done.4
  21.3 0.1 and_select_fusion.2
  21.4 0.2 convert_reduce_fusion
  21.6 0.1 compare_and_fusion.1
  21.7 7.8 %all-to-all-done = bf16[8,4,32,256]{3,2,1,0:T(8,128)(2,1)S(1)} async-done(((bf16[8,4,32,256]{3,2,1,0:T(8,128)(2,1)}), bf16[8,4,32,256]{3,2,1,0:T(8,128)(2,1)S(1)}, u32[]{:S(2)}, u32[]{:S(2)}) %all-to-all-start) | async-done | bytes 524320 | tf_op jit(solution)/shard_map/all_to_all | solution.py:81
  29.5 0.6 gather_fusion.1
  30.1 0.1 fusion.30
  30.2 0.0 copy-done.2
  30.2 0.7 pad_maximum_fusion
  30.9 0.0 all-gather.3.cloned.1.call-update
  31.0 158.9 %all-gather.3.cloned.1.call-done = bf16[2048,2304]{1,0:T(8,128)(2,1)} async-done(((bf16[32,2304]{1,0:T(8,128)(2,1)}), bf16[2048,2304]{1,0:T(8,128)(2,1)}) %all-gather.3.cloned.1.call-update) | async-done | bytes 9437200 | tf_op jit(solution)/shard_map/all_gather | solution.py:18
  189.9 8.4 %split.8 = bf16[2048,2048]{1,0:T(8,128)(2,1)} slice(bf16[2048,2304]{1,0:T(8,128)(2,1)} %all-gather.3.cloned.1.call-done), slice={[0:2048], [0:2048]} | slice | bytes 16777216 | tf_op jit(solution)/shard_map/split | solution.py:19
  198.2 12.3 %copy.49 = bf16[2048,2048]{0,1:T(8,128)(2,1)} copy(bf16[2048,2048]{1,0:T(8,128)(2,1)} %split.8) | data formatting | bytes 16777216 | tf_op jit(solution)/shard_map/reshape | solution.py:22
  210.6 6.0 %fusion.12 = f32[8,256,256]{1,2,0:T(8,128)S(1)} fusion(bf16[8,2048,256]{1,2,0:T(8,128)(2,1)} %bitcast.31, bf16[2048,2304]{1,0:T(8,128)(2,1)} %all-gather.3.cloned.1.call-done), kind=kOutput, calls=%fused_computation.17 | convolution fusion | flops 2147483648 | bytes 11534336 | tf_op jit(solution)/shard_map/pi,wpj->wij/dot_general | solution.py:93
  216.5 2.0 fusion.17
  218.5 1.9 fusion.5
  220.5 2.2 fusion.32
  222.6 2.3 fusion.3
  224.9 2.4 fusion.33
  227.3 2.2 fusion.7
  229.5 0.3 convolution_convert_fusion
  229.9 0.0 copy-done
  229.9 0.5 convolution_bitcast_fusion
  230.4 0.8 reshape.132
  231.2 8.5 %all-to-all-start.1 = ((f32[64,1,256]{2,1,0:T(1,128)}), f32[64,1,256]{2,1,0:T(1,128)S(1)}, u32[]{:S(2)}, u32[]{:S(2)}) async-start(f32[64,1,256]{2,1,0:T(1,128)} %reshape.132), calls=%async_computation.1 | async-start | bytes 131072 | tf_op jit(solution)/shard_map/all_to_all | solution.py:30
  239.6 0.0 all-gather.5.cloned.1.call-start
  239.7 0.0 copy-start.3
  239.7 6.5 %copy.52 = bf16[4,8,32,2048]{3,1,2,0:T(8,128)(2,1)} copy(bf16[4,8,32,2048]{3,2,1,0:T(8,128)(2,1)} %bitcast.36) | data formatting | bytes 8388608
  246.2 8.6 %all-to-all-done.1 = f32[64,1,256]{2,1,0:T(1,128)S(1)} async-done(((f32[64,1,256]{2,1,0:T(1,128)}), f32[64,1,256]{2,1,0:T(1,128)S(1)}, u32[]{:S(2)}, u32[]{:S(2)}) %all-to-all-start.1) | async-done | bytes 65568 | tf_op jit(solution)/shard_map/all_to_all | solution.py:30
  254.8 0.5 broadcast.151
  255.3 0.8 reduce
  256.1 0.1 reshape.133
  256.2 0.1 reduce_sum.29
  256.3 0.0 copy-start.1
  256.3 0.0 copy-done.3
  256.3 2.8 fusion
  259.2 0.0 copy-done.1
  259.2 6.0 %fusion.31 = (bf16[8,32,256]{2,1,0:T(8,128)(2,1)S(1)}, f32[8,32,256]{2,1,0:T(8,128)S(1)}) fusion(bf16[8,2048,256]{1,2,0:T(8,128)(2,1)} %bitcast.32, bf16[8,32,2048]{2,0,1:T(8,128)(2,1)S(1)} %bitcast.34), kind=kOutput, calls=%fused_computation.64 | convolution fusion | flops 268500992 | bytes 9830400 | tf_op jit(solution)/shard_map/wpq,wqi->wpi/dot_general | solution.py:114
  265.2 13.5 %all_gather.10 = bf16[8,128,256]{2,1,0:T(8,128)(2,1)} all-gather(bf16[8,32,256]{2,1,0:T(8,128)(2,1)S(1)} %get-tuple-element.4), channel_id=1, replica_groups=mesh['walk'=8,'chol_0'=16,'chol_1'=4] {'chol_1'}, dimensions={1}, use_global_device_ids=true | all-gather | bytes 655360 | tf_op jit(solution)/shard_map/all_gather | solution.py:40
  278.7 0.0 all-gather.5.cloned.1.call-update
  278.7 98.0 %all-gather.5.cloned.1.call-done = bf16[8,2048,256]{2,1,0:T(8,128)(2,1)} async-done(((bf16[8,128,256]{2,1,0:T(8,128)(2,1)}), bf16[8,2048,256]{2,1,0:T(8,128)(2,1)}) %all-gather.5.cloned.1.call-update) | async-done | bytes 8388624 | tf_op jit(solution)/shard_map/all_gather | solution.py:40
  376.7 5.6 %fusion.11 = bf16[8,32,256]{2,1,0:T(8,128)(2,1)} fusion(bf16[8,2048,256]{2,1,0:T(8,128)(2,1)} %all-gather.5.cloned.1.call-done, bf16[8,32,2048]{2,0,1:T(8,128)(2,1)S(1)} %bitcast.35, f32[8,32,256]{2,1,0:T(8,128)S(1)} %get-tuple-element.5, bf16[8,32,256]{2,1,0:T(8,128)(2,1)S(1)} %gather_fusion.1, pred[8]{0:T(512)(128)(4,1)S(1)} %get-tuple-element.2), kind=kOutput, calls=%fused_computation.14 | convolution fusion | flops 268828672 | bytes 9961480 | tf_op jit(solution)/shard_map/wpq,wqi->wpi/dot_general | solution.py:58
  (11 shorter events, 0.1 us)
Async XLA Ops:
  7.2 222.7 %copy-start = (bf16[32,32,256]{2,1,0:T(8,128)(2,1)S(1)}, bf16[32,32,256]{2,1,0:T(8,128)(2,1)}, u32[]{:S(2)}) copy-start(bf16[32,32,256]{2,1,0:T(8,128)(2,1)} %param.9) | copy-start | bytes 1572868
  7.2 14.1 %copy-start.4 = (s32[64]{0:T(128)S(1)}, s32[64]{0:T(128)}, u32[]{:S(2)}) copy-start(s32[64]{0:T(128)} %param.11) | copy-start | bytes 772
  7.2 23.0 %copy-start.2 = (bf16[32,256]{1,0:T(8,128)(2,1)S(1)}, bf16[32,256]{1,0:T(8,128)(2,1)}, u32[]{:S(2)}) copy-start(bf16[32,256]{1,0:T(8,128)(2,1)} %param.7) | copy-start | bytes 49156
  12.0 17.5 %all-to-all-start = ((bf16[8,4,32,256]{3,2,1,0:T(8,128)(2,1)}), bf16[8,4,32,256]{3,2,1,0:T(8,128)(2,1)S(1)}, u32[]{:S(2)}, u32[]{:S(2)}) async-start(bf16[8,4,32,256]{3,2,1,0:T(8,128)(2,1)} %select_select_fusion), calls=%async_computation | async-start | bytes 1048576 | tf_op jit(solution)/shard_map/all_to_all | solution.py:81
  21.3 168.6 %all-gather.3.cloned.1.call-start = ((), (), s32[]{:S(2)}) async-start(), calls=%async_computation.2 | async-start | bytes 9584640 | tf_op jit(solution)/shard_map/all_gather | solution.py:18
  231.2 23.6 %all-to-all-start.1 = ((f32[64,1,256]{2,1,0:T(1,128)}), f32[64,1,256]{2,1,0:T(1,128)S(1)}, u32[]{:S(2)}, u32[]{:S(2)}) async-start(f32[64,1,256]{2,1,0:T(1,128)} %reshape.132), calls=%async_computation.1 | async-start | bytes 131072 | tf_op jit(solution)/shard_map/all_to_all | solution.py:30
  239.6 137.1 %all-gather.5.cloned.1.call-start = ((), (), s32[]{:S(2)}) async-start(), calls=%async_computation.3 | async-start | bytes 8912896 | tf_op jit(solution)/shard_map/all_gather | solution.py:40
  239.7 16.6 %copy-start.3 = (f32[8,32]{1,0:T(8,128)S(1)}, f32[8,32]{1,0:T(8,128)}, u32[]{:S(2)}) copy-start(f32[8,32]{1,0:T(8,128)} %param.10) | copy-start | bytes 3076
  256.3 2.9 copy-start.1
Sparse Core Ops, SparseCore 0:
  31.0 158.7 all-gather.2
  278.9 97.8 all-gather.4
where the time goes:
time: 391 us; the launch traced here: 389 us
  waiting for transfers between devices  273 us (70%)
  matrix products  34.2 us (9%)
  local copies, waits for them, and re-layouts  31.2 us (8%)
  starting transfers between devices  17.8 us (5%)
  between operations  14.3 us (4%)
  blocking collectives  13.5 us (3%)
  other arithmetic  4.85 us (1%)
    all_gather x1, waiting for transfers between devices, rows_first(): out = lax.all_gather(both, axis, axis=0, tiled=True)  159 us
    all_gather x1, waiting for transfers between devices, gather_axes(): out = lax.all_gather(out, axes[number], axis=dim, tiled=True)  98 us
    all_gather x1, blocking collectives, gather_axes(): out = lax.all_gather(out, axes[number], axis=dim, tiled=True)  13.5 us
    reshape x1, local copies, waits for them, and re-layouts, rows_first(): b.reshape(-1, *t.shape[1:])  12.3 us
    all_to_all x1, starting transfers between devices, shards(): lax.all_to_all(outgoing, 'walk', split_axis=0, concat_axis=0, tiled=True)  9.25 us
    all_to_all x1, waiting for transfers between devices, copy_for_each(): return lax.all_to_all(copies, axis, split_axis=0, concat_axis=0, tiled=True)  8.63 us
    all_to_all x1, starting transfers between devices, copy_for_each(): return lax.all_to_all(copies, axis, split_axis=0, concat_axis=0, tiled=True)  8.47 us
    split x1, local copies, waits for them, and re-layouts, rows_first(): jnp.split(out, [sum(widths[:k]) for k in range(1, len(widths))], axis=1)  8.35 us
  transfers between devices with their start and end apart: 4, of which 4 were waited for; matrix products, arithmetic and copies ran while one was open for 2% of the time, Pallas kernels for 0%

commit v1 on v0

v1 whole, which is shorter than its diff:
```python
import functools

import jax
import jax.numpy as jnp
from jax import lax
from jax.experimental import pallas as pl
from jax.experimental.pallas import tpu as pltpu
from jax.sharding import PartitionSpec as P

TAU_ROOT = 0.1
Y = 4
CHUNKS = 4
LEAD = 3
F32 = jnp.float32
BF16 = jnp.bfloat16


def split_dot(a, b):
    a_hi = a.astype(BF16)
    b_hi = b.astype(BF16)
    a_lo = (a - a_hi.astype(F32)).astype(BF16)
    b_lo = (b - b_hi.astype(F32)).astype(BF16)
    dot = functools.partial(jnp.dot, preferred_element_type=F32)
    return dot(a_hi, b_hi) + (dot(a_hi, b_lo) + dot(a_lo, b_hi))


def kernel(
    groups, depth,
    source, walkers, trial, fields, rotated, cholesky,
    propagated, force_bias,
    staged, arrived, migrated, trial_rows, trial_all, walker_all, overlap,
    greens_out, greens_in, rotated_here, chol_here, bias_out, bias_y, bias_sum, bias_z,
    mixing, pot_out, pot_in, first_all, first_f32, second, result_out, result_in,
    local_sem, mig_s, mig_r, ty_s, ty_r, wy_s, wy_r, rt_s, rt_r, rw_s, rw_r,
    g_s, g_r, fy_s, fy_r, fz_s, fz_r, p_s, p_r, rf_s, rf_r, o_s, o_r,
):
    per_group, rows, electrons = walkers.shape
    vectors = fields.shape[1]
    orbitals = depth * Y * rows
    capacity = per_group // 2
    mine = per_group // Y
    block = rows * Y
    half = depth // 2
    group = lax.axis_index("walk")
    place = lax.axis_index("chol")
    z = lax.div(place, Y)
    y = lax.rem(place, Y)

    def at_y(k):
        return z * Y + lax.rem(y + k, Y)

    def at_z(k):
        return lax.rem(z + k + depth, depth) * Y + y

    def send(src, dst, s_sem, r_sem, where):
        return pltpu.make_async_remote_copy(
            src_ref=src, dst_ref=dst, send_sem=s_sem, recv_sem=r_sem,
            device_id=where, device_id_type=pl.DeviceIdType.MESH,
        )

    chol_copy = pltpu.make_async_copy(cholesky, chol_here, local_sem.at[0])
    rot_copy = pltpu.make_async_copy(rotated, rotated_here, local_sem.at[1])
    chol_copy.start()
    rot_copy.start()

    barrier = pltpu.get_barrier_semaphore()
    for k in range(1, groups):
        pl.semaphore_signal(barrier, inc=1, device_id={"walk": lax.rem(group + k, groups)},
                            device_id_type=pl.DeviceIdType.MESH)
    for k in range(1, Y):
        pl.semaphore_signal(barrier, inc=1, device_id={"chol": at_y(k)},
                            device_id_type=pl.DeviceIdType.MESH)
    for k in range(1, depth):
        pl.semaphore_signal(barrier, inc=1, device_id={"chol": at_z(k)},
                            device_id_type=pl.DeviceIdType.MESH)

    def picks(dest):
        chosen = [jnp.int32(0)] * capacity
        count = jnp.int32(0)
        for s in range(per_group):
            src = source[dest * per_group + s]
            here = lax.div(src, per_group) == group
            slot = lax.rem(src, per_group)
            for c in range(capacity):
                chosen[c] = jnp.where(here & (count == c), slot, chosen[c])
            count = count + here.astype(jnp.int32)
        return chosen

    for k in range(1, groups):
        dest = lax.rem(group + k, groups)
        for c, pick in enumerate(picks(dest)):
            staged[k, c] = walkers[pick]
    for c, pick in enumerate(picks(group)):
        arrived[group * capacity + c] = walkers[pick]

    pl.semaphore_wait(barrier, groups + Y + depth - 3)

    def mig_copy(k):
        dest = lax.rem(group + k, groups)
        return send(staged.at[k], arrived.at[pl.ds(group * capacity, capacity)],
                    mig_s.at[k], mig_r.at[k], {"walk": dest})

    def mig_arrival(k):
        origin = lax.rem(group - k + groups, groups)
        return send(staged.at[k], arrived.at[pl.ds(origin * capacity, capacity)],
                    mig_s.at[k], mig_r.at[k], {"walk": origin})

    for k in range(1, groups):
        mig_copy(k).start()

    def of_y(k):
        return lax.rem(y - k + Y, Y)

    def rows_of(owner):
        return pl.ds(pl.multiple_of(owner * rows, rows), rows)

    def ty_copy(k, owner):
        return send(trial, trial_rows.at[rows_of(owner)], ty_s.at[k], ty_r.at[k],
                    {"chol": at_y(k)})

    for k in range(1, Y):
        ty_copy(k, y).start()
    trial_rows[rows_of(y)] = trial[...]
    for k in range(1, Y):
        ty_copy(k, of_y(k)).wait_recv()
    trial_all[z] = trial_rows[...].astype(F32).T.astype(BF16)

    def forward(k, s):
        return lax.rem(z - k * s + 2 * depth, depth)

    def block_rows(origin):
        return pl.ds(pl.multiple_of(origin * block, block), block)

    def rt_copy(d, s, arriving=False):
        k = 1 if d == 0 else -1
        origin = forward(k, s + 1 if arriving else s)
        return send(trial_all.at[origin], trial_all.at[origin], rt_s.at[d, s], rt_r.at[d, s],
                    {"chol": at_z(k)})

    def ring_copy(buffer, s_sem, r_sem, d, s, c, arriving=False):
        k = 1 if d == 0 else -1
        origin = forward(k, s + 1 if arriving else s)
        part = buffer.at[c, block_rows(origin)]
        return send(part, part, s_sem.at[d, s, c], r_sem.at[d, s, c], {"chol": at_z(k)})

    steps = (half, half - 1)

    def trial_step(s):
        for d in range(2):
            if s < steps[d]:
                rt_copy(d, s, True).wait_recv()
                if s + 1 < steps[d]:
                    rt_copy(d, s + 1).start()

    def ring_step(buffer, s_sem, r_sem, s):
        for c in range(mine):
            for d in range(2):
                if s < steps[d]:
                    ring_copy(buffer, s_sem, r_sem, d, s, c, True).wait_recv()
                    if s + 1 < steps[d]:
                        ring_copy(buffer, s_sem, r_sem, d, s + 1, c).start()

    def ring_end(buffer, s_sem, r_sem):
        for d in range(2):
            for s in range(steps[d]):
                for c in range(mine):
                    ring_copy(buffer, s_sem, r_sem, d, s, c).wait_send()

    for d in range(2):
        if steps[d] > 0:
            rt_copy(d, 0).start()
    for s in range(LEAD - 1):
        trial_step(s)

    for k in range(1, groups):
        mig_arrival(k).wait_recv()
    for k in range(per_group):
        src = source[group * per_group + k]
        origin = lax.div(src, per_group)
        rank = jnp.int32(0)
        for j in range(k):
            other = lax.div(source[group * per_group + j], per_group)
            rank = rank + (other == origin).astype(jnp.int32)
        migrated[k] = arrived[origin * capacity + rank]

    def own_rows(owner):
        start = pl.multiple_of(z * block + owner * rows, rows)
        return pl.ds(start, rows)

    def wy_copy(k, owner):
        to = lax.rem(y + k, Y)
        return send(migrated.at[pl.ds(to * mine, mine)], walker_all.at[:, own_rows(owner)],
                    wy_s.at[k], wy_r.at[k], {"chol": at_y(k)})

    for k in range(1, Y):
        wy_copy(k, y).start()
    for c in range(mine):
        walker_all[c, own_rows(y)] = migrated[y * mine + c]
    trial_step(LEAD - 1)
    for k in range(1, Y):
        wy_copy(k, of_y(k)).wait_recv()
    for c in range(mine):
        for d in range(2):
            if steps[d] > 0:
                ring_copy(walker_all, rw_s, rw_r, d, 0, c).start()

    def add_overlap(origin):
        for c in range(mine):
            overlap[c] += jnp.dot(trial_all[origin], walker_all[c, block_rows(origin)],
                                  preferred_element_type=F32)

    overlap[...] = jnp.zeros_like(overlap)
    add_overlap(z)
    for s in range(half):
        ring_step(walker_all, rw_s, rw_r, s)
        trial_step(s + LEAD)
        for d in range(2):
            if s < steps[d]:
                add_overlap(forward(1 if d == 0 else -1, s + 1))

    row_id = lax.broadcasted_iota(jnp.int32, (electrons, electrons), 0)
    col_id = lax.broadcasted_iota(jnp.int32, (electrons, electrons), 1)
    identity = (row_id == col_id).astype(F32)
    for c in range(mine):
        residual = identity - overlap[c]
        squared = split_dot(residual, residual)
        fourth = split_dot(squared, squared)
        low = identity + residual
        low = low + split_dot(low, squared)
        inverse = (low + split_dot(low, fourth)).astype(BF16)
        greens_out[c] = jnp.dot(walker_all[c, block_rows(z)], inverse,
                                preferred_element_type=F32).astype(BF16)

    def turn_copy(src, dst, s_sem, r_sem, k, owner):
        to = lax.rem(y + k, Y)
        return send(src.at[:, rows_of(to)], dst.at[pl.ds(owner * mine, mine)],
                    s_sem.at[k], r_sem.at[k], {"chol": at_y(k)})

    for k in range(1, Y):
        turn_copy(greens_out, greens_in, g_s, g_r, k, y).start()
    for c in range(mine):
        greens_in[y * mine + c] = greens_out[c, rows_of(y)]
    rot_copy.wait()
    for k in range(1, Y):
        turn_copy(greens_out, greens_in, g_s, g_r, k, of_y(k)).wait_recv()

    wide = vectors * rows
    spread = lax.dot_general(
        greens_in[...].reshape(per_group * rows, electrons), rotated_here[...],
        (((1,), (1,)), ((), ())), preferred_element_type=F32,
    )
    same_row = (lax.rem(lax.broadcasted_iota(jnp.int32, (per_group * rows, wide), 0), rows)
                == lax.rem(lax.broadcasted_iota(jnp.int32, (per_group * rows, wide), 1), rows))
    picked = jnp.where(same_row, spread, 0.0).reshape(per_group, rows, wide).sum(axis=1)
    lanes = bias_out.shape[1]
    fold = (lax.div(lax.broadcasted_iota(jnp.int32, (wide, lanes), 0), rows)
            == lax.broadcasted_iota(jnp.int32, (wide, lanes), 1)).astype(F32)
    bias_out[...] = jnp.dot(picked, fold, precision=lax.Precision.HIGHEST,
                            preferred_element_type=F32)

    def fy_copy(k, owner):
        return send(bias_out, bias_y.at[owner], fy_s.at[k], fy_r.at[k], {"chol": at_y(k)})

    for k in range(1, Y):
        fy_copy(k, y).start()
    bias_y[y] = bias_out[...]
    for k in range(1, Y):
        fy_copy(k, of_y(k)).wait_recv()
    bias_sum[...] = bias_y[...].sum(axis=0)

    def fz_copy(k, owner):
        return send(bias_sum, bias_z.at[owner], fz_s.at[k], fz_r.at[k], {"chol": at_z(k)})

    for k in range(1, depth):
        fz_copy(k, z).start()
    bias_z[z] = bias_sum[...]
    for k in range(1, depth):
        fz_copy(k, lax.rem(z - k + depth, depth)).wait_recv()
    total = TAU_ROOT * bias_z[...].sum(axis=0)[:, :vectors]
    force_bias[...] = total
    shifted = (fields[...] - total).astype(BF16)

    unfold = (lax.broadcasted_iota(jnp.int32, (vectors, wide), 0)
              == lax.div(lax.broadcasted_iota(jnp.int32, (vectors, wide), 1), rows)).astype(BF16)
    stretched = jnp.dot(shifted, unfold, preferred_element_type=F32)
    stretched = jnp.broadcast_to(stretched[:, None, :], (per_group, rows, wide))
    mixing[...] = jnp.where(same_row, stretched.reshape(per_group * rows, wide), 0.0).astype(BF16)

    chol_copy.wait()
    width = orbitals // CHUNKS

    def pot_copy(k, n, owner):
        to = lax.rem(y + k, Y)
        cols = pl.ds(pl.multiple_of(n * width, width), width)
        return send(pot_out.at[pl.ds(to * mine, mine), :, cols],
                    pot_in.at[:, rows_of(owner), cols],
                    p_s.at[k, n], p_r.at[k, n], {"chol": at_y(k)})

    def pot_step(n, carry):
        cols = pl.ds(pl.multiple_of(n * width, width), width)
        made = TAU_ROOT * jnp.dot(mixing[...], chol_here[:, cols], preferred_element_type=F32)
        pot_out[:, :, cols] = made.astype(BF16).reshape(per_group, rows, width)
        for k in range(1, Y):
            pot_copy(k, n, y).start()
        for c in range(mine):
            pot_in[c, rows_of(y), cols] = pot_out[y * mine + c, :, cols]
        return carry

    lax.fori_loop(0, CHUNKS, pot_step, 0)
    for n in range(CHUNKS):
        for k in range(1, Y):
            pot_copy(k, n, of_y(k)).wait_recv()

    for c in range(mine):
        made = jnp.dot(pot_in[c], walker_all[c], preferred_element_type=F32)
        first_f32[c] = made
        first_all[c, block_rows(z)] = made.astype(BF16)
        for d in range(2):
            if steps[d] > 0:
                ring_copy(first_all, rf_s, rf_r, d, 0, c).start()

    def add_second(origin):
        for c in range(mine):
            cols = pl.ds(pl.multiple_of(origin * block, block), block)
            second[c] += jnp.dot(pot_in[c, :, cols], first_all[c, block_rows(origin)],
                                 preferred_element_type=F32)

    second[...] = jnp.zeros_like(second)
    add_second(z)
    for s in range(half):
        ring_step(first_all, rf_s, rf_r, s)
        for d in range(2):
            if s < steps[d]:
                add_second(forward(1 if d == 0 else -1, s + 1))

    for c in range(mine):
        result_out[c] = (walker_all[c, block_rows(z)].astype(F32) + first_f32[c]
                         + 0.5 * second[c]).astype(BF16)
    for k in range(1, Y):
        turn_copy(result_out, result_in, o_s, o_r, k, y).start()
    for c in range(mine):
        result_in[y * mine + c] = result_out[c, rows_of(y)]

    for k in range(1, groups):
        mig_copy(k).wait_send()
    for k in range(1, Y):
        ty_copy(k, y).wait_send()
        wy_copy(k, y).wait_send()
        turn_copy(greens_out, greens_in, g_s, g_r, k, y).wait_send()
        fy_copy(k, y).wait_send()
        for n in range(CHUNKS):
            pot_copy(k, n, y).wait_send()
    for k in range(1, depth):
        fz_copy(k, z).wait_send()
    for d in range(2):
        for s in range(steps[d]):
            rt_copy(d, s).wait_send()
    ring_end(walker_all, rw_s, rw_r)
    ring_end(first_all, rf_s, rf_r)
    for k in range(1, Y):
        turn_copy(result_out, result_in, o_s, o_r, k, of_y(k)).wait_recv()
    for k in range(1, Y):
        turn_copy(result_out, result_in, o_s, o_r, k, y).wait_send()
    propagated[...] = result_in[...]


def shards(walkers, trial, cholesky, rotated, fields, source):
    per_group, rows, electrons = walkers.shape
    vectors = rotated.shape[0]
    groups = lax.axis_size("walk")
    depth = lax.axis_size("chol") // Y
    orbitals = cholesky.shape[2]
    capacity = per_group // 2
    mine = per_group // Y
    block = rows * Y
    half = depth // 2
    wide = vectors * rows
    lanes = 128
    vmem = pltpu.VMEM
    dma = pltpu.SemaphoreType.DMA
    scratch = [
        vmem((groups, capacity, rows, electrons), BF16),
        vmem((groups * capacity, rows, electrons), BF16),
        vmem((per_group, rows, electrons), BF16),
        vmem((block, electrons), BF16),
        vmem((depth, electrons, block), BF16),
        vmem((mine, orbitals, electrons), BF16),
        vmem((mine, electrons, electrons), F32),
        vmem((mine, block, electrons), BF16),
        vmem((per_group, rows, electrons), BF16),
        vmem((wide, electrons), BF16),
        vmem((wide, orbitals), BF16),
        vmem((per_group, lanes), F32),
        vmem((Y, per_group, lanes), F32),
        vmem((per_group, lanes), F32),
        vmem((depth, per_group, lanes), F32),
        vmem((per_group * rows, wide), BF16),
        vmem((per_group, rows, orbitals), BF16),
        vmem((mine, block, orbitals), BF16),
        vmem((mine, orbitals, electrons), BF16),
        vmem((mine, block, electrons), F32),
        vmem((mine, block, electrons), F32),
        vmem((mine, block, electrons), BF16),
        vmem((per_group, rows, electrons), BF16),
        dma((2,)),
        dma((groups,)), dma((groups,)),
        dma((Y,)), dma((Y,)), dma((Y,)), dma((Y,)),
        dma((2, half)), dma((2, half)),
        dma((2, half, mine)), dma((2, half, mine)),
        dma((Y,)), dma((Y,)), dma((Y,)), dma((Y,)),
        dma((depth,)), dma((depth,)),
        dma((Y, CHUNKS)), dma((Y, CHUNKS)),
        dma((2, half, mine)), dma((2, half, mine)),
        dma((Y,)), dma((Y,)),
    ]
    in_vmem = pl.BlockSpec(memory_space=pltpu.VMEM)
    anywhere = pl.BlockSpec(memory_space=pl.ANY)
    return pl.pallas_call(
        functools.partial(kernel, groups, depth),
        out_shape=(
            jax.ShapeDtypeStruct(walkers.shape, BF16),
            jax.ShapeDtypeStruct(fields.shape, F32),
        ),
        in_specs=[pl.BlockSpec(memory_space=pltpu.SMEM), in_vmem, in_vmem, in_vmem,
                  anywhere, anywhere],
        out_specs=(in_vmem, in_vmem),
        scratch_shapes=scratch,
        compiler_params=pltpu.CompilerParams(
            collective_id=0, has_side_effects=True, vmem_limit_bytes=50 * 1024 * 1024
        ),
    )(source, walkers, trial, fields, rotated.reshape(wide, electrons),
      cholesky.reshape(wide, orbitals))


def solution(mesh):
    placed = (
        P("walk", "chol", None),
        P("chol", None),
        P(None, "chol", None),
        P(None, "chol", None),
        P("walk", None),
        P(),
    )
    return jax.shard_map(
        shards,
        mesh=mesh,
        in_specs=placed,
        out_specs=(P("walk", "chol", None), P("walk", None)),
        check_vma=False,
    )
```

time: 391 us -> 136 us (0.35)
  waiting for transfers between devices: 273 us -> 0 us
  Pallas kernels: 0 us -> 130 us
  matrix products: 34.2 us -> 0 us
  local copies, waits for them, and re-layouts: 31.2 us -> 5.25 us
  starting transfers between devices: 17.8 us -> 0 us
  between operations: 14.3 us -> 0.65 us
  blocking collectives: 13.5 us -> 0 us
  other arithmetic: 4.85 us -> 0 us
    all_gather x2 -> x0, waiting for transfers between devices: 257 us -> none  [the longest x1 159 us: rows_first(): out = lax.all_gather(both, axis, axis=0, tiled=True)]
    pallas_call x0 -> x1, Pallas kernels: none -> 130 us  [shards(): pl.pallas_call(functools.partial(kernel, groups, depth), out_shape=(jax.S...]
    dot_general x12 -> x0, matrix products: 34.2 us -> none  [the longest x3 6.52 us: newton_inverse(): jnp.einsum('wij,wjk->wik', intersections, estimate, precision=lax.Precisi...]
    all_to_all x2 -> x0, starting transfers between devices: 17.7 us -> none  [the longest x1 9.25 us: shards(): lax.all_to_all(outgoing, 'walk', split_axis=0, concat_axis=0, tiled=True)]
    all_to_all x2 -> x0, waiting for transfers between devices: 16.5 us -> none  [the longest x1 8.63 us: copy_for_each(): return lax.all_to_all(copies, axis, split_axis=0, concat_axis=0, tiled=True)]
    all_gather x1 -> x0, blocking collectives: 13.5 us -> none  [gather_axes(): out = lax.all_gather(out, axes[number], axis=dim, tiled=True)]
    reshape x3 -> x0, local copies, waits for them, and re-layouts: 12.4 us -> none  [the longest x1 12.3 us: rows_first(): b.reshape(-1, *t.shape[1:])]
    split x1 -> x0, local copies, waits for them, and re-layouts: 8.35 us -> none  [rows_first(): jnp.split(out, [sum(widths[:k]) for k in range(1, len(widths))], axis=1)]
  transfers between devices with their start and end apart: 4 -> 0, of which waited for: 4 -> 0; matrix products, arithmetic and copies ran while one was open for 2% -> 0% of each run, Pallas kernels for 0% -> 0%
where the time goes in v1:
time: 136 us
  Pallas kernels  130 us (96%)
  local copies, waits for them, and re-layouts  5.25 us (4%)
    pallas_call x1, Pallas kernels, shards(): pl.pallas_call(functools.partial(kernel, groups, depth), out_shape=(jax.S...  130 us
    unnamed x12, local copies, waits for them, and re-layouts  5.25 us

profile of v1, /device:TPU:6, one launch (start us, length us, event | category | flops | bytes accessed | tf_op | source)
XLA Modules:
  0.0 135.8 jit_solution(1997367632712662934)
XLA Ops:
  0.6 0.0 copy-start
  0.6 1.0 copy-done
  1.7 0.0 copy-start.1
  1.7 0.9 copy-done.1
  2.6 0.0 copy-start.2
  2.6 0.7 copy-done.2
  3.3 0.0 copy-start.3
  3.3 0.7 copy-done.3
  4.0 0.0 copy-start.4
  4.0 0.7 copy-done.4
  4.6 129.9 %shard_map.77 = (bf16[8,32,256]{2,1,0:T(8,128)(2,1)S(1)}, f32[8,32]{1,0:T(8,128)S(1)}) custom-call(s32[64]{0:T(128)S(1)} %copy-done.4, bf16[8,32,256]{2,1,0:T(8,128)(2,1)S(1)} %copy-done.1, bf16[32,256]{1,0:T(8,128)(2,1)S(1)} %copy-done.2, f32[8,32]{1,0:T(8,128)S(1)} %copy-done.3, bf16[1024,256]{1,0:T(8,128)(2,1)S(1)} %bitcast.2, bf16[1024,2048]{1,0:T(8,128)(2,1)} %bitcast.3), custom_call_target="tpu_custom_call" | custom-call | tf_op jit(solution)/shard_map/pallas_call | solution.py:418
  134.6 0.7 copy.10
  135.3 0.6 copy.11
Async XLA Ops:
  0.6 1.0 copy-start
  1.7 0.9 copy-start.1
  2.6 0.7 copy-start.2
  3.3 0.7 copy-start.3
  4.0 0.7 copy-start.4

commit v2 on v1

v2 whole, which is shorter than its diff:
```python
import functools

import jax
import jax.numpy as jnp
from jax import lax
from jax.experimental import pallas as pl
from jax.experimental.pallas import tpu as pltpu
from jax.sharding import PartitionSpec as P

TAU_ROOT = 0.1
Y = 8
LINE = 4
CHUNKS = 2
SUB = 4
F32 = jnp.float32
BF16 = jnp.bfloat16


def split_dot(a, b):
    a_hi = a.astype(BF16)
    b_hi = b.astype(BF16)
    a_lo = (a - a_hi.astype(F32)).astype(BF16)
    b_lo = (b - b_hi.astype(F32)).astype(BF16)
    dot = functools.partial(jnp.dot, preferred_element_type=F32)
    return dot(a_hi, b_hi) + (dot(a_hi, b_lo) + dot(a_lo, b_hi))


def kernel(
    groups, depth,
    source_far, walkers_far, trial_far, fields_far, rotated, cholesky,
    propagated, force_bias,
    source, walkers, trial, fields, staged, arrived, migrated, trial_all, trial_turned, walker_all, overlap,
    greens_out, greens_in, rotated_here, chol_here, bias_out, bias_y, bias_sum, bias_z,
    mixing, pot_out, pot_in, first_all, first_f32, second, result_out, result_in,
    local_sem, mig_s, mig_r, tz_s, tz_r, tx_s, tx_r, wy_s, wy_r, rw_s, rw_r,
    g_s, g_r, fy_s, fy_r, fz_s, fz_r, p_s, p_r, rf_s, rf_r, o_s, o_r,
):
    per_group, rows, electrons = walkers.shape
    vectors = fields.shape[1]
    orbitals = depth * Y * rows
    capacity = per_group // 2
    mine = per_group // Y
    block = rows * Y
    half = depth // 2
    strip = rows // 2
    group = lax.axis_index("walk")
    place = lax.axis_index("chol")
    z = lax.div(place, Y)
    y = lax.rem(place, Y)

    def at_y(k):
        return z * Y + lax.rem(y + k, Y)

    floors = depth * Y // LINE
    floor = lax.div(place, LINE)
    seat = lax.rem(place, LINE)

    def at_floor(k):
        return lax.rem(floor + k + floors, floors) * LINE + seat

    def at_z(k):
        return lax.rem(z + k + depth, depth) * Y + y

    def send(src, dst, s_sem, r_sem, where):
        return pltpu.make_async_remote_copy(
            src_ref=src, dst_ref=dst, send_sem=s_sem, recv_sem=r_sem,
            device_id=where, device_id_type=pl.DeviceIdType.MESH,
        )

    source_copy = pltpu.make_async_copy(source_far, source, local_sem.at[2])
    walkers_copy = pltpu.make_async_copy(walkers_far, walkers, local_sem.at[3])
    trial_copy = pltpu.make_async_copy(trial_far, trial, local_sem.at[4])
    fields_copy = pltpu.make_async_copy(fields_far, fields, local_sem.at[5])
    sent = []

    def begin(copy):
        copy.start()
        sent.append(copy)

    chol_copy = pltpu.make_async_copy(cholesky, chol_here, local_sem.at[0])
    rot_copy = pltpu.make_async_copy(rotated, rotated_here, local_sem.at[1])
    for copy in (source_copy, walkers_copy, trial_copy, fields_copy, rot_copy, chol_copy):
        copy.start()

    barrier = pltpu.get_barrier_semaphore()
    for k in range(1, groups):
        pl.semaphore_signal(barrier, inc=1, device_id={"walk": lax.rem(group + k, groups)},
                            device_id_type=pl.DeviceIdType.MESH)
    for k in range(1, Y):
        pl.semaphore_signal(barrier, inc=1, device_id={"chol": at_y(k)},
                            device_id_type=pl.DeviceIdType.MESH)
    for k in (1, -1):
        pl.semaphore_signal(barrier, inc=1, device_id={"chol": at_z(k)},
                            device_id_type=pl.DeviceIdType.MESH)
        pl.semaphore_signal(barrier, inc=1, device_id={"chol": at_floor(k)},
                            device_id_type=pl.DeviceIdType.MESH)

    source_copy.wait()
    walkers_copy.wait()
    trial_copy.wait()
    fields_copy.wait()

    def picks(dest):
        chosen = [jnp.int32(0)] * capacity
        count = jnp.int32(0)
        for s in range(per_group):
            src = source[dest * per_group + s]
            here = lax.div(src, per_group) == group
            slot = lax.rem(src, per_group)
            for c in range(capacity):
                chosen[c] = jnp.where(here & (count == c), slot, chosen[c])
            count = count + here.astype(jnp.int32)
        return chosen

    for k in range(1, groups):
        dest = lax.rem(group + k, groups)
        for c, pick in enumerate(picks(dest)):
            staged[k, c] = walkers[pick]
    for c, pick in enumerate(picks(group)):
        arrived[group * capacity + c] = walkers[pick]

    pl.semaphore_wait(barrier, groups + Y + 2)

    def mig_copy(k):
        dest = lax.rem(group + k, groups)
        return send(staged.at[k], arrived.at[pl.ds(group * capacity, capacity)],
                    mig_s.at[k], mig_r.at[k], {"walk": dest})

    def mig_arrival(k):
        origin = lax.rem(group - k + groups, groups)
        return send(staged.at[k], arrived.at[pl.ds(origin * capacity, capacity)],
                    mig_s.at[k], mig_r.at[k], {"walk": origin})

    signs = (1, -1)
    reach = (floors // 2, floors // 2 - 1)

    def tz_copy(d, q, arriving=False):
        hop = 1 if q % 2 else 2
        origin = lax.rem(floor - signs[d] * (q if arriving else q - hop) + 2 * floors, floors)
        part = trial_all.at[origin, seat]
        return send(part, part, tz_s.at[d, q - 1], tz_r.at[d, q - 1],
                    {"chol": at_floor(signs[d] * hop)})

    def trial_round(r):
        for d in range(2):
            if r > 0 and 2 * r <= reach[d]:
                tz_copy(d, 2 * r, True).wait_recv()
            for q in (2 * r + 2, 2 * r + 1):
                if q <= reach[d]:
                    begin(tz_copy(d, q))

    rounds = (floors // 2 + 1) // 2

    def trial_rest():
        for d in range(2):
            for q in range(1, reach[d] + 1):
                if q % 2 or q >= 2 * rounds:
                    tz_copy(d, q, True).wait_recv()

    def tx_copy(k, owner):
        part = trial_all.at[:, owner]
        return send(part, part, tx_s.at[k], tx_r.at[k],
                    {"chol": floor * LINE + lax.rem(seat + k, LINE)})

    trial_all[floor, seat] = trial[...]
    trial_round(0)
    for k in range(1, groups):
        begin(mig_copy(k))
    trial_round(1)

    def of_y(k):
        return lax.rem(y - k + Y, Y)

    def rows_of(owner):
        return pl.ds(pl.multiple_of(owner * rows, rows), rows)

    def forward(k, s):
        return lax.rem(z - k * s + 2 * depth, depth)

    def block_rows(origin):
        return pl.ds(pl.multiple_of(origin * block, block), block)

    piece = block // SUB

    def last(d, p):
        return half if p % 2 == d else half - 1

    def walker_part(origin, c, p):
        return walker_all.at[c, pl.ds(pl.multiple_of(origin * block + p * piece, piece), piece)]

    def ring_copy(part_of, s_sem, r_sem, d, s, c, p, arriving=False):
        part = part_of(forward(signs[d], s + 1 if arriving else s), c, p)
        at = c * SUB + p
        return send(part, part, s_sem.at[d, s, at], r_sem.at[d, s, at],
                    {"chol": at_z(signs[d])})

    def ring_start(part_of, s_sem, r_sem, c, pieces):
        for p in pieces:
            for d in range(2):
                if last(d, p) > 0:
                    begin(ring_copy(part_of, s_sem, r_sem, d, 0, c, p))

    def ring_step(part_of, s_sem, r_sem, s, use):
        for c in range(mine):
            for p in range(SUB):
                for d in range(2):
                    if s < last(d, p):
                        ring_copy(part_of, s_sem, r_sem, d, s, c, p, True).wait_recv()
                        if s + 1 < last(d, p):
                            begin(ring_copy(part_of, s_sem, r_sem, d, s + 1, c, p))
            for d in range(2 if s < half - 1 else 1):
                use(d, s, c)

    for r in range(2, rounds - 1):
        trial_round(r)
    for k in range(1, groups):
        mig_arrival(k).wait_recv()
    for k in range(per_group):
        src = source[group * per_group + k]
        origin = lax.div(src, per_group)
        rank = jnp.int32(0)
        for j in range(k):
            other = lax.div(source[group * per_group + j], per_group)
            rank = rank + (other == origin).astype(jnp.int32)
        migrated[k] = arrived[origin * capacity + rank]

    def own_rows(owner):
        start = pl.multiple_of(z * block + owner * rows, rows)
        return pl.ds(start, rows)

    def wy_copy(k, owner):
        to = lax.rem(y + k, Y)
        return send(migrated.at[pl.ds(to * mine, mine)], walker_all.at[:, own_rows(owner)],
                    wy_s.at[k], wy_r.at[k], {"chol": at_y(k)})

    for k in range(1, Y):
        begin(wy_copy(k, y))
    for c in range(mine):
        walker_all[c, own_rows(y)] = migrated[y * mine + c]
    for r in range(max(rounds - 1, 2), rounds):
        trial_round(r)
    for k in range(1, Y):
        wy_copy(k, of_y(k)).wait_recv()
    for c in range(mine):
        ring_start(walker_part, rw_s, rw_r, c, range(SUB))
    trial_rest()
    for k in range(1, LINE):
        begin(tx_copy(k, seat))

    def turn_trial(o, carry):
        rows_here = trial_all[pl.ds(o * (Y // LINE), Y // LINE)].reshape(block, electrons)
        trial_turned[o] = rows_here.astype(F32).T.astype(BF16)
        return carry

    def trial_times(origin, c):
        return jnp.dot(trial_turned[origin], walker_all[c, block_rows(origin)],
                       preferred_element_type=F32)

    pending = []

    def add_overlap(d, s, c):
        if s < turn_at:
            pending.append((d, s, c))
        else:
            overlap[c] += trial_times(forward(signs[d], s + 1), c)

    turn_at = min(2, half - 1)
    for s in range(half):
        if s == turn_at:
            for k in range(1, LINE):
                tx_copy(k, lax.rem(seat - k + LINE, LINE)).wait_recv()
            lax.fori_loop(0, depth, turn_trial, 0)
            for c in range(mine):
                overlap[c] = trial_times(z, c)
            for d, before, c in pending:
                overlap[c] += trial_times(forward(signs[d], before + 1), c)
        ring_step(walker_part, rw_s, rw_r, s, add_overlap)

    row_id = lax.broadcasted_iota(jnp.int32, (electrons, electrons), 0)
    col_id = lax.broadcasted_iota(jnp.int32, (electrons, electrons), 1)
    identity = (row_id == col_id).astype(F32)
    for c in range(mine):
        residual = identity - overlap[c]
        squared = split_dot(residual, residual)
        fourth = split_dot(squared, squared)
        low = identity + residual
        low = low + split_dot(low, squared)
        inverse = (low + split_dot(low, fourth)).astype(BF16)
        made = jnp.dot(walker_all[c, block_rows(z)], inverse, preferred_element_type=F32)
        greens_out[c] = made.astype(BF16).reshape(Y, rows, electrons)

    def turn_copy(src, dst, s_sem, r_sem, k, owner):
        to = lax.rem(y + k, Y)
        return send(src.at[:, to], dst.at[pl.ds(owner * mine, mine)],
                    s_sem.at[k], r_sem.at[k], {"chol": at_y(k)})

    for k in range(1, Y):
        begin(turn_copy(greens_out, greens_in, g_s, g_r, k, y))
    for c in range(mine):
        greens_in[y * mine + c] = greens_out[c, y]
    rot_copy.wait()
    for k in range(1, Y):
        turn_copy(greens_out, greens_in, g_s, g_r, k, of_y(k)).wait_recv()

    wide = vectors * rows
    spread = lax.dot_general(
        greens_in[...].reshape(per_group * rows, electrons), rotated_here[...],
        (((1,), (1,)), ((), ())), preferred_element_type=F32,
    )
    same_row = (lax.rem(lax.broadcasted_iota(jnp.int32, (per_group * rows, wide), 0), rows)
                == lax.rem(lax.broadcasted_iota(jnp.int32, (per_group * rows, wide), 1), rows))
    picked = jnp.where(same_row, spread, 0.0).reshape(per_group, rows, wide).sum(axis=1)
    lanes = bias_out.shape[1]
    fold = (lax.div(lax.broadcasted_iota(jnp.int32, (wide, lanes), 0), rows)
            == lax.broadcasted_iota(jnp.int32, (wide, lanes), 1)).astype(F32)
    bias_out[...] = jnp.dot(picked, fold, precision=lax.Precision.HIGHEST,
                            preferred_element_type=F32)

    def fy_copy(k, owner):
        return send(bias_out, bias_y.at[owner], fy_s.at[k], fy_r.at[k], {"chol": at_y(k)})

    for k in range(1, Y):
        begin(fy_copy(k, y))
    bias_y[y] = bias_out[...]
    for k in range(1, Y):
        fy_copy(k, of_y(k)).wait_recv()
    bias_sum[...] = bias_y[...].sum(axis=0)

    def fz_copy(k, owner):
        return send(bias_sum, bias_z.at[owner], fz_s.at[k], fz_r.at[k], {"chol": at_z(k)})

    for k in range(1, depth):
        begin(fz_copy(k, z))
    bias_z[z] = bias_sum[...]
    for k in range(1, depth):
        fz_copy(k, lax.rem(z - k + depth, depth)).wait_recv()
    total = TAU_ROOT * bias_z[...].sum(axis=0)[:, :vectors]
    force_bias[...] = total
    shifted = (fields[...] - total).astype(BF16)

    span = vectors * strip
    unfold = (lax.broadcasted_iota(jnp.int32, (vectors, span), 0)
              == lax.div(lax.broadcasted_iota(jnp.int32, (vectors, span), 1), strip)).astype(BF16)
    stretched = jnp.dot(shifted, unfold, preferred_element_type=F32)
    stretched = jnp.broadcast_to(stretched[:, None, :], (per_group, strip, span))
    kept = (lax.rem(lax.broadcasted_iota(jnp.int32, (per_group * strip, span), 0), strip)
            == lax.rem(lax.broadcasted_iota(jnp.int32, (per_group * strip, span), 1), strip))
    mixing[...] = jnp.where(kept, stretched.reshape(per_group * strip, span), 0.0).astype(BF16)

    chol_copy.wait()
    width = orbitals // CHUNKS

    def pot_copy(k, h, n, owner):
        to = lax.rem(y + k, Y)
        cols = pl.ds(n * width, width)
        return send(pot_out.at[h, pl.ds(to * mine, mine), :, cols],
                    pot_in.at[:, h, owner, :, cols],
                    p_s.at[k, h, n], p_r.at[k, h, n], {"chol": at_y(k)})

    for h in range(2):
        for n in range(CHUNKS):
            cols = pl.ds(n * width, width)
            side = chol_here[:, pl.ds(h * strip, strip), cols].reshape(span, width)
            made = TAU_ROOT * jnp.dot(mixing[...], side, preferred_element_type=F32)
            pot_out[h, :, :, cols] = made.astype(BF16).reshape(per_group, strip, width)
            for k in range(1, Y):
                begin(pot_copy(k, h, n, y))
            for c in range(mine):
                pot_in[c, h, y, :, cols] = pot_out[h, y * mine + c, :, cols]

    def first_part(origin, c, p):
        h, q = p // (SUB // 2), p % (SUB // 2)
        seats = Y // (SUB // 2)
        return first_all.at[c, origin, pl.ds(q * seats, seats), pl.ds(h * strip, strip)]

    for h in range(2):
        for n in range(CHUNKS):
            for k in range(1, Y):
                pot_copy(k, h, n, of_y(k)).wait_recv()
        for c in range(mine):
            made = jnp.dot(pot_in[c, h].reshape(Y * strip, orbitals), walker_all[c],
                           preferred_element_type=F32)
            first_f32[c, h] = made
            first_all[c, z, :, pl.ds(h * strip, strip)] = (
                made.astype(BF16).reshape(Y, strip, electrons))
            ring_start(first_part, rf_s, rf_r, c, range(h * (SUB // 2), (h + 1) * (SUB // 2)))

    def potential_times(origin, c):
        cols = pl.ds(pl.multiple_of(origin * block, block), block)
        return jnp.dot(pot_in[c, :, :, :, cols].reshape(block, block),
                       first_all[c, origin].reshape(block, electrons),
                       preferred_element_type=F32)

    def add_second(d, s, c):
        second[c] += potential_times(forward(signs[d], s + 1), c)

    for c in range(mine):
        second[c] = potential_times(z, c)
    for s in range(half):
        ring_step(first_part, rf_s, rf_r, s, add_second)

    for c in range(mine):
        own = walker_all[c, block_rows(z)].reshape(Y, rows, electrons)
        for h in range(2):
            low = own[:, h * strip:(h + 1) * strip].reshape(Y * strip, electrons).astype(F32)
            made = low + first_f32[c, h] + 0.5 * second[c, pl.ds(h * Y * strip, Y * strip)]
            result_out[c, :, pl.ds(h * strip, strip)] = (
                made.astype(BF16).reshape(Y, strip, electrons))
    for k in range(1, Y):
        begin(turn_copy(result_out, result_in, o_s, o_r, k, y))
    for c in range(mine):
        result_in[y * mine + c] = result_out[c, y]

    for k in range(1, Y):
        turn_copy(result_out, result_in, o_s, o_r, k, of_y(k)).wait_recv()
    for copy in sent:
        copy.wait_send()
    propagated[...] = result_in[...]


def shards(walkers, trial, cholesky, rotated, fields, source):
    per_group, rows, electrons = walkers.shape
    vectors = rotated.shape[0]
    groups = lax.axis_size("walk")
    depth = lax.axis_size("chol") // Y
    orbitals = cholesky.shape[2]
    capacity = per_group // 2
    mine = per_group // Y
    block = rows * Y
    half = depth // 2
    strip = rows // 2
    wide = vectors * rows
    lanes = 128
    vmem = pltpu.VMEM
    dma = pltpu.SemaphoreType.DMA
    scratch = [
        pltpu.SMEM(source.shape, jnp.int32),
        vmem(walkers.shape, BF16),
        vmem(trial.shape, BF16),
        vmem(fields.shape, F32),
        vmem((groups, capacity, rows, electrons), BF16),
        vmem((groups * capacity, rows, electrons), BF16),
        vmem((per_group, rows, electrons), BF16),
        vmem((depth * Y // LINE, LINE, rows, electrons), BF16),
        vmem((depth, electrons, block), BF16),
        vmem((mine, orbitals, electrons), BF16),
        vmem((mine, electrons, electrons), F32),
        vmem((mine, Y, rows, electrons), BF16),
        vmem((per_group, rows, electrons), BF16),
        vmem((wide, electrons), BF16),
        vmem((vectors, rows, orbitals), BF16),
        vmem((per_group, lanes), F32),
        vmem((Y, per_group, lanes), F32),
        vmem((per_group, lanes), F32),
        vmem((depth, per_group, lanes), F32),
        vmem((per_group * strip, vectors * strip), BF16),
        vmem((2, per_group, strip, orbitals), BF16),
        vmem((mine, 2, Y, strip, orbitals), BF16),
        vmem((mine, depth, Y, rows, electrons), BF16),
        vmem((mine, 2, Y * strip, electrons), F32),
        vmem((mine, block, electrons), F32),
        vmem((mine, Y, rows, electrons), BF16),
        vmem((per_group, rows, electrons), BF16),
        dma((6,)),
        dma((groups,)), dma((groups,)),
        dma((2, depth * Y // LINE // 2)), dma((2, depth * Y // LINE // 2)),
        dma((LINE,)), dma((LINE,)),
        dma((Y,)), dma((Y,)),
        dma((2, half, mine * SUB)), dma((2, half, mine * SUB)),
        dma((Y,)), dma((Y,)), dma((Y,)), dma((Y,)),
        dma((depth,)), dma((depth,)),
        dma((Y, 2, CHUNKS)), dma((Y, 2, CHUNKS)),
        dma((2, half, mine * SUB)), dma((2, half, mine * SUB)),
        dma((Y,)), dma((Y,)),
    ]
    in_vmem = pl.BlockSpec(memory_space=pltpu.VMEM)
    in_hbm = pl.BlockSpec(memory_space=pltpu.HBM)
    return pl.pallas_call(
        functools.partial(kernel, groups, depth),
        out_shape=(
            jax.ShapeDtypeStruct(walkers.shape, BF16),
            jax.ShapeDtypeStruct(fields.shape, F32),
        ),
        in_specs=[in_hbm] * 6,
        out_specs=(in_vmem, in_vmem),
        scratch_shapes=scratch,
        compiler_params=pltpu.CompilerParams(
            collective_id=0, has_side_effects=True, vmem_limit_bytes=67043328
        ),
    )(source, walkers, trial, fields, rotated.reshape(wide, electrons),
      cholesky)


def solution(mesh):
    placed = (
        P("walk", "chol", None),
        P("chol", None),
        P(None, "chol", None),
        P(None, "chol", None),
        P("walk", None),
        P(),
    )
    return jax.shard_map(
        shards,
        mesh=mesh,
        in_specs=placed,
        out_specs=(P("walk", "chol", None), P("walk", None)),
        check_vma=False,
    )
```

time: 136 us -> 116 us (0.85)
  Pallas kernels: 130 us -> 112 us
  local copies, waits for them, and re-layouts: 5.25 us -> 2.85 us
    pallas_call x1, Pallas kernels: 130 us -> 112 us  [shards(): pl.pallas_call(functools.partial(kernel, groups, depth), out_shape=(jax.S...]
    unnamed x12 -> x2, local copies, waits for them, and re-layouts: 5.25 us -> 2.85 us
where the time goes in v2:
time: 116 us; the launch traced here: 115 us
  Pallas kernels  112 us (97%)
  local copies, waits for them, and re-layouts  2.85 us (2%)
    pallas_call x1, Pallas kernels, shards(): pl.pallas_call(functools.partial(kernel, groups, depth), out_shape=(jax.S...  112 us
    unnamed x2, local copies, waits for them, and re-layouts  2.85 us

profile of v2, /device:TPU:6, one launch (start us, length us, event | category | flops | bytes accessed | tf_op | source)
XLA Modules:
  0.0 115.1 jit_solution(17928722542087045384)
XLA Ops:
  0.6 111.6 %shard_map.77 = (bf16[8,32,256]{2,1,0:T(8,128)(2,1)}, f32[8,32]{1,0:T(8,128)}) custom-call(s32[64]{0:T(128)} %source_far.1, bf16[8,32,256]{2,1,0:T(8,128)(2,1)} %walkers_far.1, bf16[32,256]{1,0:T(8,128)(2,1)} %trial_far.1, f32[8,32]{1,0:T(8,128)} %fields_far.1, bf16[1024,256]{1,0:T(8,128)(2,1)} %bitcast.1, bf16[32,32,2048]{2,1,0:T(8,128)(2,1)} %cholesky.1), custom_call_target="tpu_custom_call" | custom-call | tf_op jit(solution)/shard_map/pallas_call | solution.py:478
  112.2 1.6 %copy.10 = bf16[8,32,256]{2,1,0:T(8,128)(2,1)} copy(bf16[8,32,256]{2,1,0:T(8,128)(2,1)} %get-tuple-element.4) | data formatting | bytes 262144
  113.8 1.3 %copy.11 = f32[8,32]{1,0:T(8,128)} copy(f32[8,32]{1,0:T(8,128)} %get-tuple-element.5) | data formatting | bytes 2048

commit v3 on v2

--- a/solution.py
+++ b/solution.py
@@ -264,7 +264,7 @@
         else:
             overlap[c] += trial_times(forward(signs[d], s + 1), c)
 
-    turn_at = min(2, half - 1)
+    turn_at = half - 1
     for s in range(half):
         if s == turn_at:
             for k in range(1, LINE):
@@ -485,10 +485,10 @@
         out_specs=(in_vmem, in_vmem),
         scratch_shapes=scratch,
         compiler_params=pltpu.CompilerParams(
-            collective_id=0, has_side_effects=True, vmem_limit_bytes=67043328
+            collective_id=0, has_side_effects=True, vmem_limit_bytes=50 * 1024 * 1024
         ),
-    )(source, walkers, trial, fields, rotated.reshape(wide, electrons),
-      cholesky)
+    )(*(pltpu.with_memory_space_constraint(a, pltpu.HBM) for a in (
+        source, walkers, trial, fields, rotated.reshape(wide, electrons), cholesky)))
 
 
 def solution(mesh):

time: 116 us -> 114 us (0.983)
  local copies, waits for them, and re-layouts: 2.85 us -> 1.25 us
    unnamed x2, local copies, waits for them, and re-layouts: 2.85 us -> 1.25 us
where the time goes in v3:
time: 114 us; the launch traced here: 113 us
  Pallas kernels  111 us (97%)
  local copies, waits for them, and re-layouts  1.25 us (1%)
    pallas_call x1, Pallas kernels, shards(): pl.pallas_call(functools.partial(kernel, groups, depth), out_shape=(jax.S...  111 us

profile of v3, /device:TPU:6, one launch (start us, length us, event | category | flops | bytes accessed | tf_op | source)
XLA Modules:
  0.0 113.3 jit_solution(11230223932149846191)
XLA Ops:
  0.6 111.4 %shard_map.77 = (bf16[8,32,256]{2,1,0:T(8,128)(2,1)S(1)}, f32[8,32]{1,0:T(8,128)S(1)}) custom-call(s32[64]{0:T(128)} %source_far.1, bf16[8,32,256]{2,1,0:T(8,128)(2,1)} %walkers_far.1, bf16[32,256]{1,0:T(8,128)(2,1)} %trial_far.1, f32[8,32]{1,0:T(8,128)} %fields_far.1, bf16[1024,256]{1,0:T(8,128)(2,1)} %bitcast.1, bf16[32,32,2048]{2,1,0:T(8,128)(2,1)} %cholesky.1), custom_call_target="tpu_custom_call" | custom-call | tf_op jit(solution)/shard_map/pallas_call | solution.py:478
  112.0 0.7 copy.10
  112.7 0.6 copy.11

commit v4 on v3

--- a/solution.py
+++ b/solution.py
@@ -12,6 +12,8 @@
 LINE = 4
 CHUNKS = 2
 SUB = 4
+FAR_GROUPS = (4, 3, 5, 2, 6, 1, 7)
+FAR_SEATS = (2, 6, 1, 3, 5, 7, 4)
 F32 = jnp.float32
 BF16 = jnp.bfloat16
 
@@ -164,7 +166,7 @@
 
     trial_all[floor, seat] = trial[...]
     trial_round(0)
-    for k in range(1, groups):
+    for k in FAR_GROUPS:
         begin(mig_copy(k))
     trial_round(1)
 
@@ -233,7 +235,7 @@
         return send(migrated.at[pl.ds(to * mine, mine)], walker_all.at[:, own_rows(owner)],
                     wy_s.at[k], wy_r.at[k], {"chol": at_y(k)})
 
-    for k in range(1, Y):
+    for k in FAR_SEATS:
         begin(wy_copy(k, y))
     for c in range(mine):
         walker_all[c, own_rows(y)] = migrated[y * mine + c]
@@ -294,7 +296,7 @@
         return send(src.at[:, to], dst.at[pl.ds(owner * mine, mine)],
                     s_sem.at[k], r_sem.at[k], {"chol": at_y(k)})
 
-    for k in range(1, Y):
+    for k in FAR_SEATS:
         begin(turn_copy(greens_out, greens_in, g_s, g_r, k, y))
     for c in range(mine):
         greens_in[y * mine + c] = greens_out[c, y]
@@ -363,7 +365,7 @@
             side = chol_here[:, pl.ds(h * strip, strip), cols].reshape(span, width)
             made = TAU_ROOT * jnp.dot(mixing[...], side, preferred_element_type=F32)
             pot_out[h, :, :, cols] = made.astype(BF16).reshape(per_group, strip, width)
-            for k in range(1, Y):
+            for k in FAR_SEATS:
                 begin(pot_copy(k, h, n, y))
             for c in range(mine):
                 pot_in[c, h, y, :, cols] = pot_out[h, y * mine + c, :, cols]
@@ -406,7 +408,7 @@
             made = low + first_f32[c, h] + 0.5 * second[c, pl.ds(h * Y * strip, Y * strip)]
             result_out[c, :, pl.ds(h * strip, strip)] = (
                 made.astype(BF16).reshape(Y, strip, electrons))
-    for k in range(1, Y):
+    for k in FAR_SEATS:
         begin(turn_copy(result_out, result_in, o_s, o_r, k, y))
     for c in range(mine):
         result_in[y * mine + c] = result_out[c, y]

time: 114 us -> 113 us (level)
  no operation moved by 1% of the time
where the time goes in v4:
time: 113 us; the launch traced here: 112 us
  Pallas kernels  111 us (98%)
  local copies, waits for them, and re-layouts  1.25 us (1%)
    pallas_call x1, Pallas kernels, shards(): pl.pallas_call(functools.partial(kernel, groups, depth), out_shape=(jax.S...  111 us

profile of v4, /device:TPU:6, one launch (start us, length us, event | category | flops | bytes accessed | tf_op | source)
XLA Modules:
  0.0 112.5 jit_solution(15962723046571923922)
XLA Ops:
  0.6 110.6 %shard_map.77 = (bf16[8,32,256]{2,1,0:T(8,128)(2,1)S(1)}, f32[8,32]{1,0:T(8,128)S(1)}) custom-call(s32[64]{0:T(128)} %source_far.1, bf16[8,32,256]{2,1,0:T(8,128)(2,1)} %walkers_far.1, bf16[32,256]{1,0:T(8,128)(2,1)} %trial_far.1, f32[8,32]{1,0:T(8,128)} %fields_far.1, bf16[1024,256]{1,0:T(8,128)(2,1)} %bitcast.1, bf16[32,32,2048]{2,1,0:T(8,128)(2,1)} %cholesky.1), custom_call_target="tpu_custom_call" | custom-call | tf_op jit(solution)/shard_map/pallas_call | solution.py:480
  111.2 0.7 copy.10
  111.9 0.6 copy.11
